TPU v7x, 256 devices: a whole 4x4x8 slice. The times are simulated.
256 devices in a mesh: pair: 64 (over y, z, core), aux: 4 (over x).
Axes of the slice: x: 4, y: 4, z: 8, core: 2. Of those that a mesh axis runs over, the one named last changes fastest.
Arguments:
- factors: bfloat16 [64, 8192, 8, 128], P('pair', 'aux'), may hold values from -0.0625 to 0.0625
- amplitudes: bfloat16 [3072, 128, 128], P('pair'), may hold values from -6 to 6
- block_list: int32 [3072, 3], P('pair'), may hold values from 0 to 63, as said below
- owner_map: int32 [64], replicated, may hold values from 0 to 63, as said below
Outputs:
- residual_blocks: bfloat16 [3072, 128, 128], P('pair')
Inputs may be any that keep to these rules, and one draw needn't show every extreme that they name: `block_list`: each row (k, A, C) names an occupied orbital below 64 and two virtual blocks below 8; no row repeats. Among the 48 rows of one device at most 2 have orbitals with the same owner_map entry, and exactly 2 for some entry on every device. `owner_map`: A permutation: entry k is the row of factors that holds orbital k.
All inputs are finite; a program needn't handle non-finite values.
Results may differ from a plain program's by a relative error of at most 0.0046.
Values may be sent and summed in bfloat16 or wider, within the bound.
A program may use at most 64 MiB of HBM per device.

v0:
```python
import jax
import jax.numpy as jnp
from jax import lax
from jax.sharding import PartitionSpec as P

CAP = 2


def on_device(factors, amplitudes, block_list, owner_map):
    pair_count = lax.axis_size("pair")
    slot_total = pair_count * CAP
    block_count = amplitudes.shape[0]
    block_width = amplitudes.shape[1]
    virt_blocks = factors.shape[2]
    share_rows = factors.shape[1]
    orbital_total = owner_map.shape[0]
    orbitals = block_list[:, 0]
    block_a = block_list[:, 1]
    block_c = block_list[:, 2]
    matches = orbitals[:, None] == lax.iota(jnp.int32, orbital_total)[None, :]
    owners = jnp.sum(jnp.where(matches, owner_map[None, :], 0), axis=1)
    owner_hits = (owners[:, None] == lax.iota(jnp.int32, pair_count)[None, :]).astype(jnp.int32)
    earlier = jnp.cumsum(owner_hits, axis=0) - owner_hits
    slot_rank = jnp.sum(earlier * owner_hits, axis=1)
    slots = owners * CAP + slot_rank
    placing = slots[:, None] == lax.iota(jnp.int32, slot_total)[None, :]
    place_matrix = placing.astype(jnp.bfloat16)
    flat_blocks = amplitudes.reshape(block_count, block_width * block_width)
    send_blocks = jnp.einsum(
        "js,jm->sm", place_matrix, flat_blocks, preferred_element_type=jnp.float32
    )
    send_blocks = send_blocks.astype(jnp.bfloat16).reshape(
        pair_count, CAP, block_width, block_width
    )
    send_a = jnp.sum(jnp.where(placing, block_a[:, None] + 1, 0), axis=0)
    send_c = jnp.sum(jnp.where(placing, block_c[:, None] + 1, 0), axis=0)
    send_index = (
        jnp.stack([send_a, send_c], axis=-1).astype(jnp.bfloat16).reshape(pair_count, CAP, 2)
    )
    recv_blocks, recv_index = (
        lax.all_to_all(send_blocks, "pair", split_axis=0, concat_axis=0, tiled=True),
        lax.all_to_all(send_index, "pair", split_axis=0, concat_axis=0, tiled=True),
    )
    recv_index = recv_index.reshape(slot_total, 2).astype(jnp.int32) - 1
    slot_a = recv_index[:, 0]
    slot_c = recv_index[:, 1]
    onehot_a = (slot_a[:, None] == lax.iota(jnp.int32, virt_blocks)[None, :]).astype(jnp.bfloat16)
    onehot_c = (slot_c[:, None] == lax.iota(jnp.int32, virt_blocks)[None, :]).astype(jnp.bfloat16)
    combined = (onehot_c[:, :, None] * onehot_a[:, None, :]).reshape(
        slot_total, virt_blocks * virt_blocks
    )
    recv_flat = recv_blocks.reshape(slot_total, block_width * block_width)
    weights = jnp.einsum("sm,sn->mn", combined, recv_flat, preferred_element_type=jnp.float32)
    weights = weights.reshape(virt_blocks, virt_blocks, block_width, block_width)
    weights = jnp.transpose(weights, (0, 3, 1, 2)).reshape(
        virt_blocks * block_width, virt_blocks * block_width
    )
    weights = weights.astype(jnp.bfloat16)
    factor_flat = factors.reshape(share_rows, virt_blocks * block_width)
    factor_rows = factor_flat
    inter_share = lax.psum_scatter(
        jnp.dot(factor_rows, weights, preferred_element_type=jnp.float32),
        "pair",
        scatter_dimension=0,
        tiled=True,
    )
    inter_share = inter_share.astype(jnp.bfloat16)
    shard_rows = lax.all_gather(inter_share, "pair", axis=0, tiled=True)
    height = shard_rows.shape[0]
    factor_rows = factor_flat
    left = shard_rows.reshape(height, virt_blocks, block_width)
    right = factor_rows.reshape(height, virt_blocks, block_width)
    projected = jnp.einsum("qAa,qCc->ACac", left, right, preferred_element_type=jnp.float32)
    safe_a = jnp.maximum(slot_a, 0)
    safe_c = jnp.maximum(slot_c, 0)
    summed = lax.psum(projected, "aux")
    picked = summed[safe_a, safe_c].astype(jnp.bfloat16)
    picked = picked.reshape(pair_count, CAP, block_width, block_width)
    returned = lax.all_to_all(picked, "pair", split_axis=0, concat_axis=0, tiled=True)
    returned = returned.reshape(slot_total, block_width * block_width)
    result = jnp.einsum("js,sm->jm", place_matrix, returned, preferred_element_type=jnp.float32)
    return result.astype(jnp.bfloat16).reshape(block_count, block_width, block_width)


def solution(mesh):
    placed = (P("pair", "aux", None, None), P("pair", None, None), P("pair", None), P())
    return jax.shard_map(
        on_device, mesh=mesh, in_specs=placed, out_specs=P("pair", None, None), check_vma=False
    )
```

profile of v0, /device:TPU:1, one launch (start us, length us, event | category | flops | bytes accessed | tf_op | source)
XLA Modules:
  0.0 617.8 jit_solution(2545537378293932037)
XLA Ops:
  6.5 0.8 add_bitcast_fusion
  7.3 0.8 select_reduce_fusion.3
  8.2 0.1 fusion.18
  8.2 0.1 reduce_window_sum.11
  8.3 0.2 select_reduce_fusion.2
  8.5 0.1 select_reduce_fusion.1
  8.7 0.1 stack.10
  8.8 0.2 stack.9
  9.0 0.7 copy.26
  9.6 13.2 %all-to-all-start = ((bf16[64,2,2]{1,2,0:T(2,128)(2,1)}), bf16[64,2,2]{1,2,0:T(2,128)(2,1)S(1)}, u32[]{:S(2)}, u32[]{:S(2)}) async-start(bf16[64,2,2]{1,2,0:T(2,128)(2,1)} %copy.26), calls=%async_computation | async-start | bytes 65536 | tf_op jit(solution)/shard_map/all_to_all | solution.py:42
  22.8 2.8 fusion.10
  25.6 3.2 copy.39
  28.8 3.2 all-to-all-done
  32.0 7.3 %all-to-all-start.1 = ((bf16[64,2,128,128]{3,2,1,0:T(8,128)(2,1)}), bf16[64,2,128,128]{3,2,1,0:T(8,128)(2,1)}, u32[]{:S(2)}, u32[]{:S(2)}) async-start(bf16[64,2,128,128]{3,2,1,0:T(8,128)(2,1)} %bitcast.84), calls=%async_computation.1 | async-start | bytes 8388608 | tf_op jit(solution)/shard_map/all_to_all | solution.py:41
  39.3 0.2 reduce-scatter.4.cloned.1.call-start
  39.6 0.1 copy.27
  39.7 0.1 copy.28
  39.8 0.1 sub.11
  40.0 95.3 %all-to-all-done.1 = bf16[64,2,128,128]{3,2,1,0:T(8,128)(2,1)} async-done(((bf16[64,2,128,128]{3,2,1,0:T(8,128)(2,1)}), bf16[64,2,128,128]{3,2,1,0:T(8,128)(2,1)}, u32[]{:S(2)}, u32[]{:S(2)}) %all-to-all-start.1) | async-done | bytes 4194336 | tf_op jit(solution)/shard_map/all_to_all | solution.py:41
  135.2 7.7 %copy.70 = bf16[16,8,128,128]{3,1,2,0:T(8,128)(2,1)} copy(bf16[16,8,128,128]{3,2,1,0:T(8,128)(2,1)} %bitcast.39) | data formatting | bytes 8388608
  142.9 6.4 %copy.29 = bf16[128,16384]{0,1:T(8,128)(2,1)} copy(bf16[128,16384]{1,0:T(8,128)(2,1)} %bitcast.88) | data formatting | bytes 8388608 | tf_op jit(solution)/shard_map/reshape | solution.py:52
  149.3 3.8 convert_bitcast_fusion
  153.1 3.3 copy.30
  156.3 10.6 %convolution_bitcast_fusion = f32[2048,1024]{0,1:T(8,128)} fusion(bf16[256,8,8,128]{3,2,1,0:T(8,128)(2,1)} %bitcast.92, bf16[128,8,8,128]{3,2,1,0:T(8,128)(2,1)} %bitcast.90), kind=kOutput, calls=%fused_computation.3 | convolution fusion | flops 4294967296 | bytes 14680064 | tf_op jit(solution)/shard_map/dot_general | solution.py:62
  166.9 9.3 %copy.36 = f32[2048,1024]{1,0:T(8,128)} copy(f32[2048,1024]{0,1:T(8,128)} %convolution_bitcast_fusion) | data formatting | bytes 16777216
  176.2 0.0 reduce-scatter.4.cloned.1.call-update
  176.2 0.3 all-gather.2.cloned.1.call-start
  176.5 143.6 %reduce-scatter.4.cloned.1.call-done = f32[32,1024]{1,0:T(8,128)} async-done(((f32[2048,1024]{1,0:T(8,128)}), f32[32,1024]{1,0:T(8,128)}) %reduce-scatter.4.cloned.1.call-update) | async-done | bytes 131088 | tf_op jit(solution)/shard_map/reduce_scatter | solution.py:61
  320.2 1.5 convert_element_type.57
  321.7 0.0 all-gather.2.cloned.1.call-update
  321.7 83.6 %all-gather.2.cloned.1.call-done = bf16[2048,1024]{1,0:T(8,128)(2,1)} async-done(((bf16[32,1024]{1,0:T(8,128)(2,1)}), bf16[2048,1024]{1,0:T(8,128)(2,1)}) %all-gather.2.cloned.1.call-update) | async-done | bytes 4194320 | tf_op jit(solution)/shard_map/all_gather | solution.py:68
  405.3 6.5 %copy.32 = bf16[2048,1024]{0,1:T(8,128)(2,1)} copy(bf16[2048,1024]{1,0:T(8,128)(2,1)} %all-gather.2.cloned.1.call-done) | data formatting | bytes 8388608 | tf_op jit(solution)/shard_map/all_gather | solution.py:68
  411.8 9.9 %fusion.7 = f32[8,8,128,128]{3,2,1,0:T(8,128)} fusion(bf16[2048,8,128,1]{0,2,3,1:T(8,128)(2,1)} %bitcast.89, bf16[2048,8,128]{2,1,0:T(8,128)(2,1)} %bitcast.93), kind=kOutput, calls=%fused_computation.12 | convolution fusion | flops 4294967296 | bytes 12582912 | tf_op jit(solution)/shard_map/qAa,qCc->ACac/dot_general | solution.py:73
  421.7 78.1 %all-reduce.1 = bf16[8,8,128,128]{3,2,1,0:T(8,128)(2,1)S(1)} all-reduce(f32[8,8,128,128]{3,2,1,0:T(8,128)} %fusion.7), channel_id=1, replica_groups=mesh['pair'=64,'aux'=4] {'aux'}, use_global_device_ids=true, to_apply=%region_6.7 | all-reduce | flops 1048576 | bytes 6291456 | tf_op jit(solution)/shard_map/psum | solution.py:76
  499.8 3.1 gather_fusion
  502.8 103.9 %all_to_all.15 = bf16[64,2,128,128]{3,2,1,0:T(8,128)(2,1)S(1)} all-to-all(bf16[64,2,128,128]{3,2,1,0:T(8,128)(2,1)} %bitcast.86), channel_id=1, replica_groups=mesh['pair'=64,'aux'=4] {'pair'}, dimensions={0} | all-to-all | bytes 8388608 | tf_op jit(solution)/shard_map/all_to_all | solution.py:79
  606.7 2.7 fusion.15
  609.4 1.6 copy.44
  (7 shorter events, 0.1 us)
Async XLA Ops:
  9.6 22.4 %all-to-all-start = ((bf16[64,2,2]{1,2,0:T(2,128)(2,1)}), bf16[64,2,2]{1,2,0:T(2,128)(2,1)S(1)}, u32[]{:S(2)}, u32[]{:S(2)}) async-start(bf16[64,2,2]{1,2,0:T(2,128)(2,1)} %copy.26), calls=%async_computation | async-start | bytes 65536 | tf_op jit(solution)/shard_map/all_to_all | solution.py:42
  32.0 103.2 %all-to-all-start.1 = ((bf16[64,2,128,128]{3,2,1,0:T(8,128)(2,1)}), bf16[64,2,128,128]{3,2,1,0:T(8,128)(2,1)}, u32[]{:S(2)}, u32[]{:S(2)}) async-start(bf16[64,2,128,128]{3,2,1,0:T(8,128)(2,1)} %bitcast.84), calls=%async_computation.1 | async-start | bytes 8388608 | tf_op jit(solution)/shard_map/all_to_all | solution.py:41
  39.3 280.8 %reduce-scatter.4.cloned.1.call-start = ((), (), s32[]{:S(2)}) async-start(), calls=%async_computation.5 | async-start | bytes 8519680 | tf_op jit(solution)/shard_map/reduce_scatter | solution.py:61
  176.2 229.1 %all-gather.2.cloned.1.call-start = ((), (), s32[]{:S(2)}) async-start(), calls=%async_computation.4 | async-start | bytes 4259840 | tf_op jit(solution)/shard_map/all_gather | solution.py:68
Sparse Core Ops, SparseCore 0:
  176.4 143.7 reduce-scatter.3
  323.3 81.9 all-gather.1
where the time goes:
time: 619 us; the launch traced here: 618 us
  waiting for transfers between devices  326 us (53%)
  blocking collectives  182 us (29%)
  local copies, waits for them, and re-layouts  42.2 us (7%)
  matrix products  29.8 us (5%)
  starting transfers between devices  21 us (3%)
  between operations  13.5 us (2%)
    reduce_scatter x1, waiting for transfers between devices, on_device(): lax.psum_scatter(jnp.dot(factor_rows, weights, preferred_element_type=jnp...  144 us
    all_to_all x1, blocking collectives, on_device(): lax.all_to_all(picked, 'pair', split_axis=0, concat_axis=0, tiled=True)  104 us
    all_to_all x1, waiting for transfers between devices, on_device(): lax.all_to_all(send_blocks, 'pair', split_axis=0, concat_axis=0, tiled=True)  95.3 us
    all_gather x1, waiting for transfers between devices, on_device(): shard_rows = lax.all_gather(inter_share, 'pair', axis=0, tiled=True)  83.6 us
    psum x1, blocking collectives, on_device(): summed = lax.psum(projected, 'aux')  78.1 us
    unnamed x4, local copies, waits for them, and re-layouts  21.7 us
    all_to_all x1, starting transfers between devices, on_device(): lax.all_to_all(send_index, 'pair', split_axis=0, concat_axis=0, tiled=True)  13.2 us
  transfers between devices with their start and end apart: 4, of which 4 were waited for; matrix products, arithmetic and copies ran while one was open for 1% of the time, Pallas kernels for 0%

commit v1 on v0

--- a/solution.py
+++ b/solution.py
@@ -73,7 +73,9 @@
     projected = jnp.einsum("qAa,qCc->ACac", left, right, preferred_element_type=jnp.float32)
     safe_a = jnp.maximum(slot_a, 0)
     safe_c = jnp.maximum(slot_c, 0)
-    summed = lax.psum(projected, "aux")
+    summed = projected
+    for hop in (1, 2):
+        summed = summed + lax.ppermute(summed, "aux", [(dev, dev ^ hop) for dev in range(4)])
     picked = summed[safe_a, safe_c].astype(jnp.bfloat16)
     picked = picked.reshape(pair_count, CAP, block_width, block_width)
     returned = lax.all_to_all(picked, "pair", split_axis=0, concat_axis=0, tiled=True)

time: 619 us -> 725 us (1.17)
  waiting for transfers between devices: 326 us -> 506 us
  blocking collectives: 182 us -> 104 us
    ppermute x0 -> x2, waiting for transfers between devices: none -> 181 us  [on_device(): lax.ppermute(summed, 'aux', [(dev, dev ^ hop) for dev in range(4)])]
    psum x1 -> x0, blocking collectives: 78.1 us -> none  [on_device(): summed = lax.psum(projected, 'aux')]
  transfers between devices with their start and end apart: 4 -> 6, of which waited for: 4 -> 6; matrix products, arithmetic and copies ran while one was open for 1% -> 1% of each run, Pallas kernels for 0% -> 0%
where the time goes in v1:
time: 725 us; the launch traced here: 724 us
  waiting for transfers between devices  506 us (70%)
  blocking collectives  104 us (14%)
  local copies, waits for them, and re-layouts  42.3 us (6%)
  matrix products  27.4 us (4%)
  starting transfers between devices  25 us (3%)
  between operations  13.6 us (2%)
    ppermute x2, waiting for transfers between devices, on_device(): lax.ppermute(summed, 'aux', [(dev, dev ^ hop) for dev in range(4)])  181 us
    reduce_scatter x1, waiting for transfers between devices, on_device(): lax.psum_scatter(jnp.dot(factor_rows, weights, preferred_element_type=jnp...  144 us
    all_to_all x1, blocking collectives, on_device(): lax.all_to_all(picked, 'pair', split_axis=0, concat_axis=0, tiled=True)  104 us
    all_to_all x1, waiting for transfers between devices, on_device(): lax.all_to_all(send_blocks, 'pair', split_axis=0, concat_axis=0, tiled=True)  95.3 us
    all_gather x1, waiting for transfers between devices, on_device(): shard_rows = lax.all_gather(inter_share, 'pair', axis=0, tiled=True)  83.6 us
    unnamed x4, local copies, waits for them, and re-layouts  21.7 us
  transfers between devices with their start and end apart: 6, of which 6 were waited for; matrix products, arithmetic and copies ran while one was open for 1% of the time, Pallas kernels for 0%

profile of v1, /device:TPU:1, one launch (start us, length us, event | category | flops | bytes accessed | tf_op | source)
XLA Modules:
  0.0 724.3 jit_solution(12598169757977810213)
XLA Ops:
  6.5 0.8 add_bitcast_fusion
  7.3 0.8 select_reduce_fusion.3
  8.2 0.1 fusion.18
  8.2 0.1 reduce_window_sum.11
  8.3 0.2 select_reduce_fusion.2
  8.5 0.1 select_reduce_fusion.1
  8.7 0.1 stack.10
  8.8 0.2 stack.9
  9.0 0.7 copy.26
  9.6 13.2 %all-to-all-start = ((bf16[64,2,2]{1,2,0:T(2,128)(2,1)}), bf16[64,2,2]{1,2,0:T(2,128)(2,1)S(1)}, u32[]{:S(2)}, u32[]{:S(2)}) async-start(bf16[64,2,2]{1,2,0:T(2,128)(2,1)} %copy.26), calls=%async_computation | async-start | bytes 65536 | tf_op jit(solution)/shard_map/all_to_all | solution.py:42
  22.8 2.8 fusion.10
  25.6 3.2 copy.39
  28.8 3.2 all-to-all-done
  32.0 7.3 %all-to-all-start.1 = ((bf16[64,2,128,128]{3,2,1,0:T(8,128)(2,1)}), bf16[64,2,128,128]{3,2,1,0:T(8,128)(2,1)}, u32[]{:S(2)}, u32[]{:S(2)}) async-start(bf16[64,2,128,128]{3,2,1,0:T(8,128)(2,1)} %bitcast.84), calls=%async_computation.1 | async-start | bytes 8388608 | tf_op jit(solution)/shard_map/all_to_all | solution.py:41
  39.3 0.2 reduce-scatter.4.cloned.1.call-start
  39.6 0.1 copy.27
  39.7 0.1 copy.28
  39.8 0.1 sub.11
  40.0 95.3 %all-to-all-done.1 = bf16[64,2,128,128]{3,2,1,0:T(8,128)(2,1)} async-done(((bf16[64,2,128,128]{3,2,1,0:T(8,128)(2,1)}), bf16[64,2,128,128]{3,2,1,0:T(8,128)(2,1)}, u32[]{:S(2)}, u32[]{:S(2)}) %all-to-all-start.1) | async-done | bytes 4194336 | tf_op jit(solution)/shard_map/all_to_all | solution.py:41
  135.2 7.7 %copy.70 = bf16[16,8,128,128]{3,1,2,0:T(8,128)(2,1)} copy(bf16[16,8,128,128]{3,2,1,0:T(8,128)(2,1)} %bitcast.39) | data formatting | bytes 8388608
  142.9 6.4 copy.29
  149.3 3.8 convert_bitcast_fusion
  153.1 3.3 copy.30
  156.3 10.6 %convolution_bitcast_fusion = f32[2048,1024]{0,1:T(8,128)} fusion(bf16[256,8,8,128]{3,2,1,0:T(8,128)(2,1)} %bitcast.92, bf16[128,8,8,128]{3,2,1,0:T(8,128)(2,1)} %bitcast.90), kind=kOutput, calls=%fused_computation.3 | convolution fusion | flops 4294967296 | bytes 14680064 | tf_op jit(solution)/shard_map/dot_general | solution.py:62
  166.9 9.3 %copy.36 = f32[2048,1024]{1,0:T(8,128)} copy(f32[2048,1024]{0,1:T(8,128)} %convolution_bitcast_fusion) | data formatting | bytes 16777216
  176.2 0.0 reduce-scatter.4.cloned.1.call-update
  176.2 0.3 all-gather.2.cloned.1.call-start
  176.5 143.6 %reduce-scatter.4.cloned.1.call-done = f32[32,1024]{1,0:T(8,128)} async-done(((f32[2048,1024]{1,0:T(8,128)}), f32[32,1024]{1,0:T(8,128)}) %reduce-scatter.4.cloned.1.call-update) | async-done | bytes 131088 | tf_op jit(solution)/shard_map/reduce_scatter | solution.py:61
  320.2 1.5 convert_element_type.57
  321.7 0.0 all-gather.2.cloned.1.call-update
  321.7 83.6 %all-gather.2.cloned.1.call-done = bf16[2048,1024]{1,0:T(8,128)(2,1)} async-done(((bf16[32,1024]{1,0:T(8,128)(2,1)}), bf16[2048,1024]{1,0:T(8,128)(2,1)}) %all-gather.2.cloned.1.call-update) | async-done | bytes 4194320 | tf_op jit(solution)/shard_map/all_gather | solution.py:68
  405.4 6.5 copy.32
  411.9 7.5 %fusion.7 = f32[8,8,128,128]{3,2,1,0:T(8,128)S(1)} fusion(bf16[2048,8,128,1]{0,2,3,1:T(8,128)(2,1)} %bitcast.89, bf16[2048,8,128]{2,1,0:T(8,128)(2,1)} %bitcast.93), kind=kOutput, calls=%fused_computation.12 | convolution fusion | flops 4294967296 | bytes 12582912 | tf_op jit(solution)/shard_map/qAa,qCc->ACac/dot_general | solution.py:73
  419.4 1.3 collective-permute-start
  420.7 90.7 %collective-permute-done = f32[8,8,128,128]{3,2,1,0:T(8,128)S(1)} collective-permute-done((f32[8,8,128,128]{3,2,1,0:T(8,128)S(1)}, f32[8,8,128,128]{3,2,1,0:T(8,128)S(1)}, u32[]{:S(2)}, u32[]{:S(2)}) %collective-permute-start) | collective-permute-done | bytes 4194336 | tf_op jit(solution)/shard_map/ppermute | solution.py:78
  511.4 1.1 add.28
  512.5 2.8 collective-permute-start.1
  515.3 89.8 %collective-permute-done.1 = f32[8,8,128,128]{3,2,1,0:T(8,128)S(1)} collective-permute-done((f32[8,8,128,128]{3,2,1,0:T(8,128)S(1)}, f32[8,8,128,128]{3,2,1,0:T(8,128)S(1)}, u32[]{:S(2)}, u32[]{:S(2)}) %collective-permute-start.1) | collective-permute-done | bytes 4194336 | tf_op jit(solution)/shard_map/ppermute | solution.py:78
  605.1 0.9 add.29
  606.0 3.1 gather_fusion
  609.0 104.2 %all_to_all.15 = bf16[64,2,128,128]{3,2,1,0:T(8,128)(2,1)S(1)} all-to-all(bf16[64,2,128,128]{3,2,1,0:T(8,128)(2,1)} %bitcast.86), channel_id=1, replica_groups=mesh['pair'=64,'aux'=4] {'pair'}, dimensions={0} | all-to-all | bytes 8388608 | tf_op jit(solution)/shard_map/all_to_all | solution.py:81
  713.2 2.7 fusion.15
  716.0 1.6 copy.44
  (7 shorter events, 0.1 us)
Async XLA Ops:
  9.6 22.4 %all-to-all-start = ((bf16[64,2,2]{1,2,0:T(2,128)(2,1)}), bf16[64,2,2]{1,2,0:T(2,128)(2,1)S(1)}, u32[]{:S(2)}, u32[]{:S(2)}) async-start(bf16[64,2,2]{1,2,0:T(2,128)(2,1)} %copy.26), calls=%async_computation | async-start | bytes 65536 | tf_op jit(solution)/shard_map/all_to_all | solution.py:42
  32.0 103.2 %all-to-all-start.1 = ((bf16[64,2,128,128]{3,2,1,0:T(8,128)(2,1)}), bf16[64,2,128,128]{3,2,1,0:T(8,128)(2,1)}, u32[]{:S(2)}, u32[]{:S(2)}) async-start(bf16[64,2,128,128]{3,2,1,0:T(8,128)(2,1)} %bitcast.84), calls=%async_computation.1 | async-start | bytes 8388608 | tf_op jit(solution)/shard_map/all_to_all | solution.py:41
  39.3 280.8 %reduce-scatter.4.cloned.1.call-start = ((), (), s32[]{:S(2)}) async-start(), calls=%async_computation.5 | async-start | bytes 8519680 | tf_op jit(solution)/shard_map/reduce_scatter | solution.py:61
  176.2 229.1 %all-gather.2.cloned.1.call-start = ((), (), s32[]{:S(2)}) async-start(), calls=%async_computation.4 | async-start | bytes 4259840 | tf_op jit(solution)/shard_map/all_gather | solution.py:68
  419.4 92.0 %collective-permute-start = (f32[8,8,128,128]{3,2,1,0:T(8,128)S(1)}, f32[8,8,128,128]{3,2,1,0:T(8,128)S(1)}, u32[]{:S(2)}, u32[]{:S(2)}) collective-permute-start(f32[8,8,128,128]{3,2,1,0:T(8,128)S(1)} %fusion.7), channel_id=1, source_target_pairs={{0,1},{1,0},{2,3},{3,2},{4,5},{5,4},{6,7},{7,6},{8,9},{9,8},{10,11... | collective-permute-start | bytes 12582920 | tf_op jit(solution)/shard_map/ppermute | solution.py:78
  512.5 92.6 %collective-permute-start.1 = (f32[8,8,128,128]{3,2,1,0:T(8,128)S(1)}, f32[8,8,128,128]{3,2,1,0:T(8,128)S(1)}, u32[]{:S(2)}, u32[]{:S(2)}) collective-permute-start(f32[8,8,128,128]{3,2,1,0:T(8,128)S(1)} %add.28), channel_id=1, source_target_pairs={{0,2},{1,3},{2,0},{3,1},{4,6},{5,7},{6,4},{7,5},{8,10},{9,11},{10,... | collective-permute-start | bytes 12582920 | tf_op jit(solution)/shard_map/ppermute | solution.py:78
Sparse Core Ops, SparseCore 0:
  176.4 143.7 reduce-scatter.3
  323.3 82.0 all-gather.1
